TPU v7x, 32 devices: a whole 2x2x4 slice. The times are simulated.
32 devices in a mesh: req: 2 (over y), ctx: 8 (over z, x), tp: 2 (over core).
Axes of the slice: x: 2, y: 2, z: 4, core: 2. Of those that a mesh axis runs over, the one named last changes fastest.
Arguments:
- queries: bfloat16 [32, 5120], P(('req', 'ctx'), 'tp'), parts along dimension 0, may hold values from -9 to 9, as said below
- repeat_block_keys: bfloat16 [32, 1024], P(('req', 'ctx'), 'tp'), parts along dimension 0, may hold values from -12 to 12
- context_keys: bfloat16 [16384, 1024], P(('req', 'ctx'), 'tp'), parts along dimension 0, may hold values from -15 to 15, as said below
Outputs:
- importance: float32 [8, 16384], P('tp', ('req', 'ctx')), parts along dimension 1
There are 2 independent parts, one for each index of `req`. A program takes and returns all parts, laid end to end along the dimension named above; each array names one. Nothing has to cross between parts.
Inputs may be any that keep to these rules, and one draw needn't show every extreme that they name: queries of order one. `context_keys`: cached keys of order one.
All inputs are finite; a program needn't handle non-finite values.
Results may differ from a plain program's by a relative error of at most 0.0003.
Values may be sent and summed in bfloat16 or wider, within the bound.
A program may use at most 64 MiB of HBM per device.

v0:
```python
import math

import jax
import jax.numpy as jnp
from jax import lax
from jax.sharding import PartitionSpec as P

HEAD_SIZE = 128


NEG_FILL = -1e30


def head_scores(query_head, key_head, score_scale):
    return (
        lax.dot_general(
            query_head, key_head, (((1,), (1,)), ((), ())), preferred_element_type=jnp.float32
        )
        * score_scale
    )


def on_device(queries, repeat_block_keys, context_keys):
    cache_len = context_keys.shape[0]
    kv_heads = context_keys.shape[1] // HEAD_SIZE
    q_heads = queries.shape[1] // HEAD_SIZE
    group = q_heads // kv_heads
    score_scale = 1.0 / math.sqrt(HEAD_SIZE)
    gathered, gathered_keys = (
        lax.all_gather(queries, "ctx", axis=0, tiled=True),
        lax.all_gather(repeat_block_keys, "ctx", axis=0, tiled=True),
    )
    all_rows = gathered.shape[0]
    group_rows = group * all_rows
    query_groups = (
        gathered.reshape(all_rows, kv_heads, group, HEAD_SIZE)
        .transpose(1, 2, 0, 3)
        .reshape(kv_heads, group_rows, HEAD_SIZE)
    )
    cache_heads = context_keys.reshape(cache_len, kv_heads, HEAD_SIZE).transpose(1, 0, 2)
    row_index = jnp.arange(all_rows, dtype=jnp.int32)

    def local_stats(kv_head):
        query_block = query_groups[kv_head]
        scores = head_scores(query_block, cache_heads[kv_head], score_scale)
        local_max = jnp.max(scores, axis=1)
        local_sum = jnp.sum(jnp.exp(scores - local_max[:, None]), axis=1)
        return (local_max, local_sum)

    local_max, local_sum = lax.map(local_stats, jnp.arange(kv_heads))
    global_max = lax.pmax(local_max, "ctx")
    global_sum = lax.psum(local_sum * jnp.exp(local_max - global_max), "ctx")
    span_heads = gathered_keys.reshape(all_rows, kv_heads, HEAD_SIZE).transpose(1, 0, 2)
    causal = jnp.tile(row_index[None, :] <= row_index[:, None], (group, 1))

    def self_stats(kv_head):
        scores = jnp.where(
            causal, head_scores(query_groups[kv_head], span_heads[kv_head], score_scale), NEG_FILL
        )
        self_max = jnp.max(scores, axis=1)
        return (self_max, jnp.sum(jnp.exp(scores - self_max[:, None]), axis=1))

    self_max, self_sum = lax.map(self_stats, jnp.arange(kv_heads))
    joined = jnp.maximum(global_max, self_max)
    global_sum = global_sum * jnp.exp(global_max - joined) + self_sum * jnp.exp(self_max - joined)
    global_max = joined
    log_shift = global_max + jnp.log(global_sum)

    def group_importance(kv_head):
        scores = head_scores(query_groups[kv_head], cache_heads[kv_head], score_scale)
        return jnp.max(scores - log_shift[kv_head][:, None], axis=0)

    return lax.map(group_importance, jnp.arange(kv_heads))


def solution(mesh):
    placed = (P(("req", "ctx"), "tp"), P(("req", "ctx"), "tp"), P(("req", "ctx"), "tp"))
    return jax.shard_map(
        on_device, mesh=mesh, in_specs=placed, out_specs=P("tp", ("req", "ctx")), check_vma=False
    )
```

profile of v0, /device:TPU:0, one launch (start us, length us, event | category | flops | bytes accessed | tf_op | source)
XLA Modules:
  0.0 142.9 jit_solution(6211169349459594682)
XLA Ops:
  0.0 32.6 %all-gather = bf16[8,2,2560]{2,1,0:T(2,128)(2,1)S(1)} all-gather(bf16[1,2,2560]{2,1,0:T(2,128)(2,1)} %bitcast.85), channel_id=1, replica_groups=mesh['req'=2,'ctx'=8,'tp'=2] {'ctx'}, dimensions={0}, use_global_device_ids=true | all-gather | bytes 92160 | tf_op jit(solution)/shard_map/all_gather | solution.py:30
  32.6 0.1 reshape.30
  32.7 1.5 %copy.15 = bf16[1024,512]{0,1:T(8,128)(2,1)S(1)} copy(bf16[1024,512]{1,0:T(8,128)(2,1)} %param.11) | data formatting | bytes 2097152 | tf_op args[2]
  34.2 0.7 copy.18
  34.9 13.4 %while.35 = (s32[]{:T(128)}, f32[4,80]{1,0:T(4,128)S(1)}, f32[4,80]{1,0:T(4,128)S(1)}, s32[4]{0:T(128)S(1)}, bf16[4,80,128]{2,1,0:T(8,128)(2,1)S(1)}, /*index=5*...) while((s32[]{:T(128)}, f32[4,80]{1,0:T(4,128)S(1)}, f32[4,80]{1,0:T(4,128)S(1)}, ...), condition=%wide.region_3.4_spmd, body=%wide.region_0.3_spmd.sunk | while | flops 21299044 | bytes 941395 | solution.py:50
  34.9 0.7 dynamic_slice.81
  37.6 0.3 fusion.31
  38.0 0.2 exponential_reduce_fusion.4
  38.3 0.7 dynamic_slice.81
  41.0 0.3 fusion.31
  41.3 0.2 exponential_reduce_fusion.4
  41.6 0.7 dynamic_slice.81
  44.3 0.3 fusion.31
  44.7 0.2 exponential_reduce_fusion.4
  45.0 0.7 dynamic_slice.81
  47.7 0.3 fusion.31
  48.0 0.2 exponential_reduce_fusion.4
  48.3 21.3 %pmax.7 = f32[4,80]{1,0:T(4,128)S(1)} all-reduce(f32[4,80]{1,0:T(4,128)S(1)} %get-tuple-element.108), channel_id=1, replica_groups=mesh['req'=2,'ctx'=8,'tp'=2] {'ctx'}, use_global_device_ids=true, to_apply=%region_4.5 | all-reduce | flops 320 | bytes 2560 | tf_op jit(solution)/shard_map/pmax | solution.py:51
  69.6 0.0 copy-start
  69.6 17.1 %psum.7 = f32[4,80]{1,0:T(4,128)S(1)} all-reduce(f32[4,80]{1,0:T(4,128)S(1)} %exponential_multiply_fusion), channel_id=1, replica_groups=mesh['req'=2,'ctx'=8,'tp'=2] {'ctx'}, use_global_device_ids=true, to_apply=%region_9.10 | all-reduce | flops 320 | bytes 2560 | tf_op jit(solution)/shard_map/psum | solution.py:52
  86.8 0.0 copy-done
  86.8 26.1 %all-gather.1 = bf16[8,2,512]{2,1,0:T(2,128)(2,1)S(1)} all-gather(bf16[1,2,512]{2,1,0:T(2,128)(2,1)S(1)} %bitcast.86), channel_id=1, replica_groups=mesh['req'=2,'ctx'=8,'tp'=2] {'ctx'}, dimensions={0}, use_global_device_ids=true | all-gather | bytes 18432 | tf_op jit(solution)/shard_map/all_gather | solution.py:31
  113.0 12.5 %while.37 = (s32[]{:T(128)}, f32[4,80]{1,0:T(4,128)S(1)}, f32[4,80]{1,0:T(4,128)S(1)}, s32[4]{0:T(128)S(1)}, bf16[4,80,128]{2,1,0:T(8,128)(2,1)S(1)}, /*index=5*...) while((s32[]{:T(128)}, f32[4,80]{1,0:T(4,128)S(1)}, ...), condition=%wide.region_8.9_spmd.clone, body=%wide.region_5.0_spmd.clone.sunk | while | flops 333925 | bytes 44379 | solution.py:63
  113.0 0.7 dynamic_slice.88
  115.7 0.1 tile.22
  115.8 0.1 fusion.36
  116.1 0.7 dynamic_slice.88
  118.8 0.1 tile.22
  118.9 0.1 fusion.36
  119.2 0.7 dynamic_slice.88
  122.0 0.1 tile.22
  122.0 0.1 fusion.36
  122.3 0.7 dynamic_slice.88
  125.1 0.1 tile.22
  125.2 0.1 fusion.36
  125.5 17.4 %while.36 = (s32[]{:T(128)}, f32[4,1024]{1,0:T(4,128)}, s32[4]{0:T(128)S(1)}, bf16[4,80,128]{2,1,0:T(8,128)(2,1)S(1)}, bf16[4,1024,128]{2,1,0:T(8,128)(2,1)S(1)}...) while((s32[]{:T(128)}, f32[4,1024]{1,0:T(4,128)}, s32[4]{0:T(128)S(1)}, ...), condition=%wide.region_12.13_spmd, body=%wide.region_10.12_spmd.sunk | while | flops 21216260 | bytes 297235 | solution.py:73
  125.5 0.7 dynamic_slice.85
  128.2 0.2 fusion.35
  128.5 1.4 dynamic_update_slice.26
  129.8 0.7 dynamic_slice.85
  132.6 0.2 fusion.35
  132.8 1.4 dynamic_update_slice.26
  134.2 0.7 dynamic_slice.85
  136.9 0.2 fusion.35
  137.2 1.4 dynamic_update_slice.26
  138.5 0.7 dynamic_slice.85
  141.3 0.2 fusion.35
  141.5 1.4 dynamic_update_slice.26
  (42 shorter events, 0.9 us)
Async XLA Ops:
  69.6 17.1 %copy-start = (bf16[2,512]{1,0:T(2,128)(2,1)S(1)}, bf16[2,512]{1,0:T(2,128)(2,1)}, u32[]{:S(2)}) copy-start(bf16[2,512]{1,0:T(2,128)(2,1)} %param.10) | copy-start | bytes 6148
where the time goes:
time: 144 us; the launch traced here: 143 us
  blocking collectives  97.1 us (67%)
  loops' own time  25.1 us (17%)
  local copies, waits for them, and re-layouts  16.8 us (12%)
  matrix products  2.75 us (2%)
    all_gather x1, blocking collectives, on_device(): lax.all_gather(queries, 'ctx', axis=0, tiled=True)  32.6 us
    all_gather x1, blocking collectives, on_device(): lax.all_gather(repeat_block_keys, 'ctx', axis=0, tiled=True)  26.1 us
    pmax x1, blocking collectives, on_device(): global_max = lax.pmax(local_max, 'ctx')  21.3 us
    psum x1, blocking collectives, on_device(): global_sum = lax.psum(local_sum * jnp.exp(local_max - global_max), 'ctx')  17.1 us
    another operation x1, loops' own time, on_device(): self_max, self_sum = lax.map(self_stats, jnp.arange(kv_heads))  8.4 us
    another operation x1, loops' own time, on_device(): return lax.map(group_importance, jnp.arange(kv_heads))  8.38 us
    another operation x1, loops' own time, on_device(): local_max, local_sum = lax.map(local_stats, jnp.arange(kv_heads))  8.34 us
    dynamic_slice x12, local copies, waits for them, and re-layouts, on_device(): local_max, local_sum = lax.map(local_stats, jnp.arange(kv_heads))  7.98 us

commit v1 on v0

v1 whole, which is shorter than its diff:
```python
import functools
import math

import jax
import jax.numpy as jnp
from jax import lax
from jax.experimental import pallas as pl
from jax.experimental.pallas import tpu as pltpu
from jax.sharding import PartitionSpec as P

HEAD_SIZE = 128
LANES = 128
BLOCK_ROWS = 16
NEG_FILL = -1e30
SCALE = 1.0 / math.sqrt(HEAD_SIZE)
EXP2_SCALE = SCALE * math.log2(math.e)
NT = (((1,), (1,)), ((), ()))


def kernel(
    n, group, q_ref, own_ref, k_ref, out_ref,
    q_all, own, keys, q_block, scores, lse,
    q_send, q_recv, l_send, l_recv, local_sem,
):
    me = lax.axis_index("ctx")
    per = q_ref.shape[0]
    kv_heads = k_ref.shape[1] // HEAD_SIZE
    peers_per_block = BLOCK_ROWS // per
    blocks = n // peers_per_block
    used = group * BLOCK_ROWS
    peer = lambda offset: lax.rem(me + offset, n)

    load_keys = pltpu.make_async_copy(k_ref, keys, local_sem.at[0])
    load_own = pltpu.make_async_copy(own_ref, own, local_sem.at[1])
    load_q = pltpu.make_async_copy(q_ref, q_all.at[me], local_sem.at[2])

    barrier = pltpu.get_barrier_semaphore()
    for offset in range(1, n):
        pl.semaphore_signal(
            barrier, inc=1, device_id={"ctx": peer(offset)}, device_id_type=pl.DeviceIdType.MESH
        )
    load_keys.start()
    load_own.start()
    load_q.start()
    pl.semaphore_wait(barrier, n - 1)

    def send_q(offset, slot):
        return pltpu.make_async_remote_copy(
            src_ref=q_ref,
            dst_ref=q_all.at[slot],
            send_sem=q_send.at[offset - 1],
            recv_sem=q_recv.at[offset - 1],
            device_id={"ctx": peer(offset)},
            device_id_type=pl.DeviceIdType.MESH,
        )

    def send_lse(offset, slot):
        return pltpu.make_async_remote_copy(
            src_ref=lse.at[slot],
            dst_ref=lse.at[slot],
            send_sem=l_send.at[offset - 1],
            recv_sem=l_recv.at[offset - 1],
            device_id={"ctx": peer(offset)},
            device_id_type=pl.DeviceIdType.MESH,
        )

    for offset in range(1, n):
        send_q(offset, me).start()
    load_own.wait()
    load_keys.wait()
    load_q.wait()
    for offset in range(1, n):
        send_q(offset, peer(n - offset)).wait_recv()

    def each_block(body):
        if blocks == 1:
            body(0)
        else:
            lax.fori_loop(0, blocks, lambda b, c: (body(b), c)[1], 0)

    def queries_of(head):
        return jnp.concatenate(
            [
                q_block[:, (head * group + u) * HEAD_SIZE : (head * group + u + 1) * HEAD_SIZE]
                for u in range(group)
            ],
            axis=0,
        ).astype(jnp.bfloat16)

    def gather_block(b):
        for p in range(peers_per_block):
            q_block[p * per : (p + 1) * per, :] = q_all[b * peers_per_block + p].astype(jnp.float32)

    def stats(b):
        gather_block(b)
        lane = lax.broadcasted_iota(jnp.int32, (per, LANES), 1)
        row = b * BLOCK_ROWS + lax.rem(lane, BLOCK_ROWS)
        column = me * per + lax.broadcasted_iota(jnp.int32, (per, LANES), 0)
        causal = column <= row
        pad = jnp.zeros((LANES - used, HEAD_SIZE), jnp.bfloat16)
        for head in range(kv_heads):
            at = slice(head * HEAD_SIZE, (head + 1) * HEAD_SIZE)
            q = jnp.concatenate([queries_of(head), pad], axis=0)
            s = lax.dot_general(keys[:, at], q, NT, preferred_element_type=jnp.float32)
            t = lax.dot_general(own[:, at], q, NT, preferred_element_type=jnp.float32)
            t = jnp.where(causal, t, NEG_FILL)
            top = jnp.maximum(
                jnp.max(s, axis=0, keepdims=True), jnp.max(t, axis=0, keepdims=True)
            )
            total = jnp.sum(jnp.exp2((s - top) * EXP2_SCALE), axis=0, keepdims=True)
            total += jnp.sum(jnp.exp2((t - top) * EXP2_SCALE), axis=0, keepdims=True)
            lse[me, b, head : head + 1, :] = top * SCALE + jnp.log(total)

    lse[me] = jnp.zeros(lse.shape[1:], jnp.float32)
    each_block(stats)
    for offset in range(1, n):
        send_lse(offset, me).start()

    def keep_scores(b):
        if blocks > 1:
            gather_block(b)
        for head in range(kv_heads):
            at = slice(head * HEAD_SIZE, (head + 1) * HEAD_SIZE)
            scores[b, head] = lax.dot_general(
                queries_of(head), keys[:, at], NT, preferred_element_type=jnp.float32
            )

    each_block(keep_scores)
    for offset in range(1, n):
        send_lse(offset, peer(n - offset)).wait_recv()

    out_ref[...] = jnp.full(out_ref.shape, -jnp.inf, jnp.float32)

    def finish(b):
        parts = lse[:, b]
        top = jnp.max(parts, axis=0)
        shift = top + jnp.log(jnp.sum(jnp.exp(parts - top[None]), axis=0))
        columns = jnp.transpose(shift)
        for head in range(kv_heads):
            best = jnp.max(
                scores[b, head] * SCALE - columns[:used, head : head + 1], axis=0, keepdims=True
            )
            out_ref[head : head + 1, :] = jnp.maximum(out_ref[head : head + 1, :], best)

    each_block(finish)
    for offset in range(1, n):
        send_q(offset, me).wait_send()
        send_lse(offset, me).wait_send()


def solution(mesh):
    n = mesh.shape["ctx"]

    def on_device(queries, repeat_block_keys, context_keys):
        per, width = queries.shape
        cache_len, key_width = context_keys.shape
        kv_heads = key_width // HEAD_SIZE
        group = width // key_width
        blocks = n * per // BLOCK_ROWS
        assert blocks * BLOCK_ROWS == n * per
        return pl.pallas_call(
            functools.partial(kernel, n, group),
            out_shape=jax.ShapeDtypeStruct((kv_heads, cache_len), jnp.float32),
            in_specs=[pl.BlockSpec(memory_space=pl.ANY)] * 3,
            out_specs=pl.BlockSpec(memory_space=pltpu.VMEM),
            scratch_shapes=[
                pltpu.VMEM((n, per, width), jnp.bfloat16),
                pltpu.VMEM((per, key_width), jnp.bfloat16),
                pltpu.VMEM((cache_len, key_width), jnp.bfloat16),
                pltpu.VMEM((BLOCK_ROWS, width), jnp.float32),
                pltpu.VMEM((blocks, kv_heads, group * BLOCK_ROWS, cache_len), jnp.float32),
                pltpu.VMEM((n, blocks, 8, LANES), jnp.float32),
                pltpu.SemaphoreType.DMA((n - 1,)),
                pltpu.SemaphoreType.DMA((n - 1,)),
                pltpu.SemaphoreType.DMA((n - 1,)),
                pltpu.SemaphoreType.DMA((n - 1,)),
                pltpu.SemaphoreType.DMA((3,)),
            ],
            compiler_params=pltpu.CompilerParams(collective_id=0, has_side_effects=True),
        )(queries, repeat_block_keys, context_keys)

    placed = (P(("req", "ctx"), "tp"), P(("req", "ctx"), "tp"), P(("req", "ctx"), "tp"))
    return jax.shard_map(
        on_device, mesh=mesh, in_specs=placed, out_specs=P("tp", ("req", "ctx")), check_vma=False
    )
```

time: 144 us -> 18.4 us (0.13)
  blocking collectives: 97.1 us -> 0 us
  loops' own time: 25.1 us -> 0 us
  Pallas kernels: 0 us -> 16.8 us
  local copies, waits for them, and re-layouts: 16.8 us -> 1.32 us
  matrix products: 2.75 us -> 0 us
    all_gather x2 -> x0, blocking collectives: 58.7 us -> none  [the longest x1 32.6 us: on_device(): lax.all_gather(queries, 'ctx', axis=0, tiled=True)]
    another operation x3 -> x0, loops' own time: 25.1 us -> none  [the longest x1 8.4 us: on_device(): self_max, self_sum = lax.map(self_stats, jnp.arange(kv_heads))]
    pmax x1 -> x0, blocking collectives: 21.3 us -> none  [on_device(): global_max = lax.pmax(local_max, 'ctx')]
    psum x1 -> x0, blocking collectives: 17.1 us -> none  [on_device(): global_sum = lax.psum(local_sum * jnp.exp(local_max - global_max), 'ctx')]
    pallas_call x0 -> x1, Pallas kernels: none -> 16.8 us  [on_device(): pl.pallas_call(functools.partial(kernel, n, group), out_shape=jax.ShapeDt...]
    dynamic_slice x12 -> x0, local copies, waits for them, and re-layouts: 7.98 us -> none  [on_device(): local_max, local_sum = lax.map(local_stats, jnp.arange(kv_heads))]
    dynamic_update_slice x20 -> x0, local copies, waits for them, and re-layouts: 6.01 us -> none  [the longest x4 5.43 us: on_device(): return lax.map(group_importance, jnp.arange(kv_heads))]
    dot_general x12 -> x0, matrix products: 2.75 us -> none  [head_scores(): lax.dot_general(query_head, key_head, (((1,), (1,)), ((), ())), preferred...]
where the time goes in v1:
time: 18.4 us; the launch traced here: 18.1 us
  Pallas kernels  16.8 us (91%)
  local copies, waits for them, and re-layouts  1.32 us (7%)
    pallas_call x1, Pallas kernels, on_device(): pl.pallas_call(functools.partial(kernel, n, group), out_shape=jax.ShapeDt...  16.8 us
    unnamed x1, local copies, waits for them, and re-layouts  1.32 us

profile of v1, /device:TPU:0, one launch (start us, length us, event | category | flops | bytes accessed | tf_op | source)
XLA Modules:
  0.0 18.1 jit_solution(17411393746982742351)
XLA Ops:
  0.0 16.8 %shard_map.37 = f32[4,1024]{1,0:T(4,128)} custom-call(bf16[2,2560]{1,0:T(2,128)(2,1)} %q_ref.1, bf16[2,512]{1,0:T(2,128)(2,1)} %own_ref.1, bf16[1024,512]{1,0:T(8,128)(2,1)} %k_ref.1), custom_call_target="tpu_custom_call" | custom-call | tf_op jit(solution)/shard_map/pallas_call | solution.py:161
  16.8 1.3 %copy.5 = f32[4,1024]{1,0:T(4,128)} copy(f32[4,1024]{1,0:T(4,128)} %shard_map.37) | data formatting | bytes 32768

commit v2 on v1

--- a/solution.py
+++ b/solution.py
@@ -12,14 +12,16 @@
 LANES = 128
 BLOCK_ROWS = 16
 NEG_FILL = -1e30
+RESIDENT_BYTES = 2 << 20
+RESIDENT_LIMIT = 8 << 20
 SCALE = 1.0 / math.sqrt(HEAD_SIZE)
 EXP2_SCALE = SCALE * math.log2(math.e)
 NT = (((1,), (1,)), ((), ()))
 
 
 def kernel(
-    n, group, q_ref, own_ref, k_ref, out_ref,
-    q_all, own, keys, q_block, scores, lse,
+    n, group, q_ref, own_ref, k_ref, scores, lse,
+    q_all, own, keys, q_block,
     q_send, q_recv, l_send, l_recv, local_sem,
 ):
     me = lax.axis_index("ctx")
@@ -28,14 +30,15 @@
     peers_per_block = BLOCK_ROWS // per
     blocks = n // peers_per_block
     used = group * BLOCK_ROWS
-    peer = lambda offset: lax.rem(me + offset, n)
+    turn = 1 - 2 * (me // (n // 2))
+    peer = lambda offset: lax.rem(me + turn * offset + n, n)
 
     load_keys = pltpu.make_async_copy(k_ref, keys, local_sem.at[0])
     load_own = pltpu.make_async_copy(own_ref, own, local_sem.at[1])
     load_q = pltpu.make_async_copy(q_ref, q_all.at[me], local_sem.at[2])
 
     barrier = pltpu.get_barrier_semaphore()
-    for offset in range(1, n):
+    for offset in reversed(range(1, n)):
         pl.semaphore_signal(
             barrier, inc=1, device_id={"ctx": peer(offset)}, device_id_type=pl.DeviceIdType.MESH
         )
@@ -49,7 +52,7 @@
             src_ref=q_ref,
             dst_ref=q_all.at[slot],
             send_sem=q_send.at[offset - 1],
-            recv_sem=q_recv.at[offset - 1],
+            recv_sem=q_recv.at[slot],
             device_id={"ctx": peer(offset)},
             device_id_type=pl.DeviceIdType.MESH,
         )
@@ -59,18 +62,18 @@
             src_ref=lse.at[slot],
             dst_ref=lse.at[slot],
             send_sem=l_send.at[offset - 1],
-            recv_sem=l_recv.at[offset - 1],
+            recv_sem=l_recv.at[slot],
             device_id={"ctx": peer(offset)},
             device_id_type=pl.DeviceIdType.MESH,
         )
 
-    for offset in range(1, n):
+    for offset in reversed(range(1, n)):
         send_q(offset, me).start()
     load_own.wait()
     load_keys.wait()
     load_q.wait()
     for offset in range(1, n):
-        send_q(offset, peer(n - offset)).wait_recv()
+        send_q(offset, peer(offset)).wait_recv()
 
     def each_block(body):
         if blocks == 1:
@@ -113,7 +116,7 @@
 
     lse[me] = jnp.zeros(lse.shape[1:], jnp.float32)
     each_block(stats)
-    for offset in range(1, n):
+    for offset in reversed(range(1, n)):
         send_lse(offset, me).start()
 
     def keep_scores(b):
@@ -127,8 +130,15 @@
 
     each_block(keep_scores)
     for offset in range(1, n):
-        send_lse(offset, peer(n - offset)).wait_recv()
-
+        send_lse(offset, peer(offset)).wait_recv()
+
+    for offset in range(1, n):
+        send_q(offset, me).wait_send()
+        send_lse(offset, me).wait_send()
+
+
+def finish_kernel(scores, lse, out_ref):
+    blocks, kv_heads, used, _ = scores.shape
     out_ref[...] = jnp.full(out_ref.shape, -jnp.inf, jnp.float32)
 
     def finish(b):
@@ -142,10 +152,10 @@
             )
             out_ref[head : head + 1, :] = jnp.maximum(out_ref[head : head + 1, :], best)
 
-    each_block(finish)
-    for offset in range(1, n):
-        send_q(offset, me).wait_send()
-        send_lse(offset, me).wait_send()
+    if blocks == 1:
+        finish(0)
+    else:
+        lax.fori_loop(0, blocks, lambda b, c: (finish(b), c)[1], 0)
 
 
 def solution(mesh):
@@ -158,26 +168,38 @@
         group = width // key_width
         blocks = n * per // BLOCK_ROWS
         assert blocks * BLOCK_ROWS == n * per
-        return pl.pallas_call(
+        held_bytes = 4 * blocks * kv_heads * group * BLOCK_ROWS * cache_len
+        resident = held_bytes <= RESIDENT_BYTES
+        held = pltpu.VMEM if resident else jax.ShapeDtypeStruct
+        finish_limit = RESIDENT_LIMIT if resident else None
+        scores, lse = pl.pallas_call(
             functools.partial(kernel, n, group),
-            out_shape=jax.ShapeDtypeStruct((kv_heads, cache_len), jnp.float32),
+            out_shape=[
+                held((blocks, kv_heads, group * BLOCK_ROWS, cache_len), jnp.float32),
+                held((n, blocks, 8, LANES), jnp.float32),
+            ],
             in_specs=[pl.BlockSpec(memory_space=pl.ANY)] * 3,
-            out_specs=pl.BlockSpec(memory_space=pltpu.VMEM),
+            out_specs=[pl.BlockSpec(memory_space=pltpu.VMEM)] * 2,
             scratch_shapes=[
                 pltpu.VMEM((n, per, width), jnp.bfloat16),
                 pltpu.VMEM((per, key_width), jnp.bfloat16),
                 pltpu.VMEM((cache_len, key_width), jnp.bfloat16),
                 pltpu.VMEM((BLOCK_ROWS, width), jnp.float32),
-                pltpu.VMEM((blocks, kv_heads, group * BLOCK_ROWS, cache_len), jnp.float32),
-                pltpu.VMEM((n, blocks, 8, LANES), jnp.float32),
-                pltpu.SemaphoreType.DMA((n - 1,)),
-                pltpu.SemaphoreType.DMA((n - 1,)),
-                pltpu.SemaphoreType.DMA((n - 1,)),
-                pltpu.SemaphoreType.DMA((n - 1,)),
+                pltpu.SemaphoreType.DMA((n,)),
+                pltpu.SemaphoreType.DMA((n,)),
+                pltpu.SemaphoreType.DMA((n,)),
+                pltpu.SemaphoreType.DMA((n,)),
                 pltpu.SemaphoreType.DMA((3,)),
             ],
             compiler_params=pltpu.CompilerParams(collective_id=0, has_side_effects=True),
         )(queries, repeat_block_keys, context_keys)
+        return pl.pallas_call(
+            finish_kernel,
+            out_shape=jax.ShapeDtypeStruct((kv_heads, cache_len), jnp.float32),
+            in_specs=[pl.BlockSpec(memory_space=pltpu.VMEM)] * 2,
+            out_specs=pl.BlockSpec(memory_space=pltpu.VMEM),
+            compiler_params=pltpu.CompilerParams(vmem_limit_bytes=finish_limit),
+        )(scores, lse)
 
     placed = (P(("req", "ctx"), "tp"), P(("req", "ctx"), "tp"), P(("req", "ctx"), "tp"))
     return jax.shard_map(

time: 18.4 us -> 16.4 us (0.89)
  local copies, waits for them, and re-layouts: 1.32 us -> 0 us
  Pallas kernels: 16.8 us -> 16.3 us
    unnamed x1 -> x0, local copies, waits for them, and re-layouts: 1.32 us -> none
    pallas_call x1 -> x2, Pallas kernels: 16.8 us -> 16.3 us  [the longest x1 15.3 us: on_device(): pl.pallas_call(functools.partial(kernel, n, group), out_shape=[held((bloc...]
where the time goes in v2:
time: 16.4 us; the launch traced here: 16.3 us
  Pallas kernels  16.3 us (99%)
    pallas_call x1, Pallas kernels, on_device(): pl.pallas_call(functools.partial(kernel, n, group), out_shape=[held((bloc...  15.3 us
    pallas_call x1, Pallas kernels, on_device(): pl.pallas_call(finish_kernel, out_shape=jax.ShapeDtypeStruct((kv_heads, c...  0.94 us

profile of v2, /device:TPU:0, one launch (start us, length us, event | category | flops | bytes accessed | tf_op | source)
XLA Modules:
  0.0 16.3 jit_solution(15992074615886300140)
XLA Ops:
  0.0 15.3 %shard_map.37 = (f32[1,4,80,1024]{3,2,1,0:T(8,128)S(1)}, f32[8,1,8,128]{3,2,1,0:T(8,128)S(1)}) custom-call(bf16[2,2560]{1,0:T(2,128)(2,1)} %q_ref.1, bf16[2,512]{1,0:T(2,128)(2,1)} %own_ref.1, bf16[1024,512]{1,0:T(8,128)(2,1)} %k_ref.1), custom_call_target="tpu_custom_call" | custom-call | tf_op jit(solution)/shard_map/pallas_call | solution.py:175
  15.3 0.9 %shard_map.38 = f32[4,1024]{1,0:T(4,128)} custom-call(f32[1,4,80,1024]{3,2,1,0:T(8,128)S(1)} %get-tuple-element.7.scores, f32[8,1,8,128]{3,2,1,0:T(8,128)S(1)} %get-tuple-element.8.lse), custom_call_target="tpu_custom_call" | custom-call | tf_op jit(solution)/shard_map/pallas_call | solution.py:196

commit v3 on v2

--- a/solution.py
+++ b/solution.py
@@ -42,14 +42,15 @@
         pl.semaphore_signal(
             barrier, inc=1, device_id={"ctx": peer(offset)}, device_id_type=pl.DeviceIdType.MESH
         )
+    load_q.start()
+    load_own.start()
     load_keys.start()
-    load_own.start()
-    load_q.start()
+    load_q.wait()
     pl.semaphore_wait(barrier, n - 1)
 
     def send_q(offset, slot):
         return pltpu.make_async_remote_copy(
-            src_ref=q_ref,
+            src_ref=q_all.at[me],
             dst_ref=q_all.at[slot],
             send_sem=q_send.at[offset - 1],
             recv_sem=q_recv.at[slot],
@@ -71,7 +72,6 @@
         send_q(offset, me).start()
     load_own.wait()
     load_keys.wait()
-    load_q.wait()
     for offset in range(1, n):
         send_q(offset, peer(offset)).wait_recv()
 

time: 16.4 us -> 16.3 us (level)
  Pallas kernels: 16.3 us -> 16 us
    pallas_call x1, Pallas kernels: 15.3 us -> 15.1 us  [on_device(): pl.pallas_call(functools.partial(kernel, n, group), out_shape=[held((bloc...]
where the time goes in v3:
time: 16.3 us; the launch traced here: 16.1 us
  Pallas kernels  16 us (98%)
    pallas_call x1, Pallas kernels, on_device(): pl.pallas_call(functools.partial(kernel, n, group), out_shape=[held((bloc...  15.1 us
    pallas_call x1, Pallas kernels, on_device(): pl.pallas_call(finish_kernel, out_shape=jax.ShapeDtypeStruct((kv_heads, c...  0.94 us

profile of v3, /device:TPU:0, one launch (start us, length us, event | category | flops | bytes accessed | tf_op | source)
XLA Modules:
  0.0 16.1 jit_solution(11090049937179577986)
XLA Ops:
  0.0 15.1 %shard_map.37 = (f32[1,4,80,1024]{3,2,1,0:T(8,128)S(1)}, f32[8,1,8,128]{3,2,1,0:T(8,128)S(1)}) custom-call(bf16[2,2560]{1,0:T(2,128)(2,1)} %q_ref.1, bf16[2,512]{1,0:T(2,128)(2,1)} %own_ref.1, bf16[1024,512]{1,0:T(8,128)(2,1)} %k_ref.1), custom_call_target="tpu_custom_call" | custom-call | tf_op jit(solution)/shard_map/pallas_call | solution.py:175
  15.1 0.9 %shard_map.38 = f32[4,1024]{1,0:T(4,128)} custom-call(f32[1,4,80,1024]{3,2,1,0:T(8,128)S(1)} %get-tuple-element.7.scores, f32[8,1,8,128]{3,2,1,0:T(8,128)S(1)} %get-tuple-element.8.lse), custom_call_target="tpu_custom_call" | custom-call | tf_op jit(solution)/shard_map/pallas_call | solution.py:196

commit v4 on v3

--- a/solution.py
+++ b/solution.py
@@ -52,9 +52,19 @@
         return pltpu.make_async_remote_copy(
             src_ref=q_all.at[me],
             dst_ref=q_all.at[slot],
-            send_sem=q_send.at[offset - 1],
-            recv_sem=q_recv.at[slot],
+            send_sem=q_send,
+            recv_sem=q_recv,
             device_id={"ctx": peer(offset)},
+            device_id_type=pl.DeviceIdType.MESH,
+        )
+
+    def everyone(slots, send, recv):
+        return pltpu.make_async_remote_copy(
+            src_ref=slots.at[pl.ds(0, n - 1)],
+            dst_ref=slots.at[pl.ds(0, n - 1)],
+            send_sem=send,
+            recv_sem=recv,
+            device_id={"ctx": peer(1)},
             device_id_type=pl.DeviceIdType.MESH,
         )
 
@@ -62,8 +72,8 @@
         return pltpu.make_async_remote_copy(
             src_ref=lse.at[slot],
             dst_ref=lse.at[slot],
-            send_sem=l_send.at[offset - 1],
-            recv_sem=l_recv.at[slot],
+            send_sem=l_send,
+            recv_sem=l_recv,
             device_id={"ctx": peer(offset)},
             device_id_type=pl.DeviceIdType.MESH,
         )
@@ -72,8 +82,7 @@
         send_q(offset, me).start()
     load_own.wait()
     load_keys.wait()
-    for offset in range(1, n):
-        send_q(offset, peer(offset)).wait_recv()
+    everyone(q_all, q_send, q_recv).wait_recv()
 
     def each_block(body):
         if blocks == 1:
@@ -129,12 +138,10 @@
             )
 
     each_block(keep_scores)
-    for offset in range(1, n):
-        send_lse(offset, peer(offset)).wait_recv()
-
-    for offset in range(1, n):
-        send_q(offset, me).wait_send()
-        send_lse(offset, me).wait_send()
+    everyone(lse, l_send, l_recv).wait_recv()
+
+    everyone(q_all, q_send, q_recv).wait_send()
+    everyone(lse, l_send, l_recv).wait_send()
 
 
 def finish_kernel(scores, lse, out_ref):
@@ -185,10 +192,10 @@
                 pltpu.VMEM((per, key_width), jnp.bfloat16),
                 pltpu.VMEM((cache_len, key_width), jnp.bfloat16),
                 pltpu.VMEM((BLOCK_ROWS, width), jnp.float32),
-                pltpu.SemaphoreType.DMA((n,)),
-                pltpu.SemaphoreType.DMA((n,)),
-                pltpu.SemaphoreType.DMA((n,)),
-                pltpu.SemaphoreType.DMA((n,)),
+                pltpu.SemaphoreType.DMA,
+                pltpu.SemaphoreType.DMA,
+                pltpu.SemaphoreType.DMA,
+                pltpu.SemaphoreType.DMA,
                 pltpu.SemaphoreType.DMA((3,)),
             ],
             compiler_params=pltpu.CompilerParams(collective_id=0, has_side_effects=True),

time: 16.3 us -> 16 us (0.982)
  Pallas kernels: 16 us -> 15.8 us
    pallas_call x1, Pallas kernels: 15.1 us -> 14.8 us  [on_device(): pl.pallas_call(functools.partial(kernel, n, group), out_shape=[held((bloc...]
where the time goes in v4:
time: 16 us; the launch traced here: 15.8 us
  Pallas kernels  15.8 us (99%)
    pallas_call x1, Pallas kernels, on_device(): pl.pallas_call(functools.partial(kernel, n, group), out_shape=[held((bloc...  14.8 us
    pallas_call x1, Pallas kernels, on_device(): pl.pallas_call(finish_kernel, out_shape=jax.ShapeDtypeStruct((kv_heads, c...  0.94 us

profile of v4, /device:TPU:0, one launch (start us, length us, event | category | flops | bytes accessed | tf_op | source)
XLA Modules:
  0.0 15.8 jit_solution(6736483701689166247)
XLA Ops:
  0.0 14.8 %shard_map.37 = (f32[1,4,80,1024]{3,2,1,0:T(8,128)S(1)}, f32[8,1,8,128]{3,2,1,0:T(8,128)S(1)}) custom-call(bf16[2,2560]{1,0:T(2,128)(2,1)} %q_ref.1, bf16[2,512]{1,0:T(2,128)(2,1)} %own_ref.1, bf16[1024,512]{1,0:T(8,128)(2,1)} %k_ref.1), custom_call_target="tpu_custom_call" | custom-call | tf_op jit(solution)/shard_map/pallas_call | solution.py:182
  14.8 0.9 %shard_map.38 = f32[4,1024]{1,0:T(4,128)} custom-call(f32[1,4,80,1024]{3,2,1,0:T(8,128)S(1)} %get-tuple-element.7.scores, f32[8,1,8,128]{3,2,1,0:T(8,128)S(1)} %get-tuple-element.8.lse), custom_call_target="tpu_custom_call" | custom-call | tf_op jit(solution)/shard_map/pallas_call | solution.py:203
